TPU v7x, 32 devices: a whole 2x2x4 slice. The times are simulated.
32 devices in a mesh: fsdp: 2 (over x), ctx: 4 (over z), tp: 4 (over y, core).
Axes of the slice: x: 2, y: 2, z: 4, core: 2. Of those that a mesh axis runs over, the one named last changes fastest.
Arguments:
- inputs: bfloat16 [2, 1024, 2048], P('fsdp', 'ctx'), may hold values from -6 to 6
- attn_gain: bfloat16 [2048], P(('fsdp', 'ctx')), may hold values from 0.099609375 to 1.8984375
- qkv_weight: bfloat16 [2048, 3, 2048], P(('fsdp', 'ctx'), None, 'tp'), may hold values from -0.125 to 0.125
- out_weight: bfloat16 [2048, 2048], P(('fsdp', 'ctx'), 'tp'), may hold values from -1 to 1
- qk_gains: bfloat16 [2, 2048], P(None, 'tp'), may hold values from 0.099609375 to 1.8984375
- mlp_gain: bfloat16 [2048], P(('fsdp', 'ctx')), may hold values from 0.099609375 to 1.8984375
- router_weight: bfloat16 [2048, 8], P(('fsdp', 'ctx')), may hold values from -0.0625 to 0.0625
- gate_up_weight: bfloat16 [2048, 2, 8, 1024], P(('fsdp', 'ctx'), None, None, 'tp'), may hold values from -0.125 to 0.125
- down_weight: bfloat16 [2048, 8, 1024], P(('fsdp', 'ctx'), None, 'tp'), may hold values from -1.5 to 1.5
- routes: int32 [4, 2, 256, 4], P('ctx', 'fsdp'), may hold values from 0 to 7, all different within a row; in each aligned block of 256 rows (0 to 255, 256 to 511, ..., all dimensions but the last counted through in order) at most 160 rows name the same one
- cotangent: bfloat16 [2, 1024, 2048], P('fsdp', 'ctx'), may hold values from -6 to 6
Outputs:
- output: bfloat16 [2, 1024, 2048], P('fsdp', 'ctx')
- grad_inputs: float32 [2, 1024, 2048], P('fsdp', 'ctx')
- grad_attn_gain: float32 [2048], P(('fsdp', 'ctx'))
- grad_qkv: float32 [2048, 3, 2048], P(('fsdp', 'ctx'), None, 'tp')
- grad_out: float32 [2048, 2048], P(('fsdp', 'ctx'), 'tp')
- grad_qk_gains: float32 [2, 2048], P(None, 'tp')
- grad_mlp_gain: float32 [2048], P(('fsdp', 'ctx'))
- grad_router: float32 [2048, 8], P(('fsdp', 'ctx'))
- grad_gate_up: float32 [2048, 2, 8, 1024], P(('fsdp', 'ctx'), None, None, 'tp')
- grad_down: float32 [2048, 8, 1024], P(('fsdp', 'ctx'), None, 'tp')
Inputs may be any that keep to these rules, and one draw needn't show every extreme that they name: `routes`: each row names 4 different experts. Among the 256 tokens of one device (aligned blocks of the array in its order) no expert is named more than 160 times, a bound that some block reaches.
All inputs are finite; a program needn't handle non-finite values.
Results may differ from a plain program's by a relative error of at most 0.017.
Values may be sent and summed in bfloat16 or wider, within the bound.
A program may use at most 256 MiB of HBM per device.

v0:
```python
import math
import jax
import jax.numpy as jnp
from jax import lax
from jax.sharding import PartitionSpec as P

HEAD_DIM = 128
TOPK = 4
EXPERTS = 8
HQ = 2048
CAP = 160
epsilon = 1e-05
highest = lax.Precision.HIGHEST


def inv_rms(values):
    return lax.rsqrt(jnp.mean(values * values, axis=-1, keepdims=True) + epsilon)


def rotary_tables(offset, length):
    half_dim = HEAD_DIM // 2
    frequency = jnp.exp(
        jnp.arange(half_dim, dtype=jnp.float32) * (-2.0 * math.log(10000.0) / HEAD_DIM)
    )
    positions = (offset + jnp.arange(length, dtype=jnp.int32)).astype(jnp.float32)
    angles = positions[:, None] * frequency[None, :]
    angles = jnp.concatenate([angles, angles], axis=1)
    return (jnp.cos(angles), jnp.sin(angles))


def rotate(values, cosine, sine_table):
    half_dim = values.shape[-1] // 2
    turned = jnp.concatenate([-values[..., half_dim:], values[..., :half_dim]], axis=-1)
    return values * cosine + turned * sine_table


def rotate_back(grads, cosine, sine_table):
    half_dim = grads.shape[-1] // 2
    scaled = grads * sine_table
    return grads * cosine + jnp.concatenate(
        [scaled[..., half_dim:], -scaled[..., :half_dim]], axis=-1
    )


def slot_table(routed):
    flat_routes = routed.reshape(-1)
    one_hot = (flat_routes[:, None] == jnp.arange(EXPERTS, dtype=jnp.int32)[None, :]).astype(
        jnp.int32
    )
    earlier = jnp.cumsum(one_hot, axis=0) - one_hot
    within = jnp.sum(earlier * one_hot, axis=1)
    slots = flat_routes * CAP + within
    owners = jnp.arange(flat_routes.shape[0], dtype=jnp.int32) // TOPK
    token_of = jnp.zeros((EXPERTS * CAP,), jnp.int32).at[slots].set(owners)
    filled = jnp.zeros((EXPERTS * CAP,), jnp.float32).at[slots].set(1.0)
    return (slots.reshape(routed.shape), token_of, filled)


def on_device(
    inputs,
    attn_gain,
    qkv_weight,
    out_weight,
    qk_gains,
    mlp_gain,
    router_weight,
    gate_up_weight,
    down_weight,
    routes,
    cotangent,
):
    seq_dev, block, width = inputs.shape
    rows = seq_dev * block
    heads_dev = qkv_weight.shape[2] // HEAD_DIM
    scale = 1.0 / math.sqrt(HEAD_DIM)
    place = lax.axis_index("ctx")
    attn_gain_all, qkv_all, out_all, mlp_gain_all, router_all = (
        lax.all_gather(attn_gain, ("fsdp", "ctx"), axis=0, tiled=True),
        lax.all_gather(qkv_weight, ("fsdp", "ctx"), axis=0, tiled=True),
        lax.all_gather(out_weight, ("fsdp", "ctx"), axis=0, tiled=True),
        lax.all_gather(mlp_gain, ("fsdp", "ctx"), axis=0, tiled=True),
        lax.all_gather(router_weight, ("fsdp", "ctx"), axis=0, tiled=True),
    )
    attn_scale = attn_gain_all.astype(jnp.float32)
    mlp_scale = mlp_gain_all.astype(jnp.float32)
    flat_in = inputs.reshape(rows, width).astype(jnp.float32)
    first_rms = inv_rms(flat_in)
    normed = (flat_in * first_rms * attn_scale).astype(jnp.bfloat16)
    projected = jnp.einsum("td,dch->tch", normed, qkv_all, preferred_element_type=jnp.float32)
    query_proj = projected[:, 0]
    key_proj = projected[:, 1]
    query_sums, key_sums = lax.psum(
        (jnp.sum(query_proj * query_proj, axis=-1), jnp.sum(key_proj * key_proj, axis=-1)), "tp"
    )
    query_rms = lax.rsqrt(query_sums / HQ + epsilon)[:, None]
    key_rms = lax.rsqrt(key_sums / HQ + epsilon)[:, None]
    query_gain = qk_gains[0].astype(jnp.float32)
    key_gain = qk_gains[1].astype(jnp.float32)
    query_norm = query_proj * query_rms * query_gain
    key_norm = key_proj * key_rms * key_gain
    cosine, sine_table = rotary_tables(place * block, block)
    cos_heads = cosine[:, None, :]
    sin_heads = sine_table[:, None, :]
    head_shape = (seq_dev, block, heads_dev, HEAD_DIM)
    query_rot = rotate(query_norm.reshape(head_shape), cos_heads, sin_heads).astype(jnp.bfloat16)
    key_rot = rotate(key_norm.reshape(head_shape), cos_heads, sin_heads).astype(jnp.bfloat16)
    value_heads = projected[:, 2].reshape(head_shape).astype(jnp.bfloat16)
    key_all, value_all = (
        lax.all_gather(key_rot, "ctx", axis=1, tiled=True),
        lax.all_gather(value_heads, "ctx", axis=1, tiled=True),
    )
    length = key_all.shape[1]
    key_block = jnp.arange(length, dtype=jnp.int32) // block
    allowed = (key_block <= place)[None, None, None, :]
    scores = (
        jnp.einsum("sqhd,skhd->shqk", query_rot, key_all, preferred_element_type=jnp.float32)
        * scale
    )
    scores = jnp.where(allowed, scores, -1e30)
    top_score = jnp.max(scores, axis=-1, keepdims=True)
    exponent = jnp.exp(scores - top_score)
    total = jnp.sum(exponent, axis=-1, keepdims=True)
    log_total = top_score + jnp.log(total)
    softmaxed = exponent / total
    attended = jnp.einsum(
        "shqk,skhd->sqhd",
        softmaxed.astype(jnp.bfloat16),
        value_all,
        preferred_element_type=jnp.float32,
    )
    attended = attended.reshape(rows, heads_dev * HEAD_DIM).astype(jnp.bfloat16)
    branch = lax.psum(
        jnp.einsum("th,dh->td", attended, out_all, preferred_element_type=jnp.float32), "tp"
    )
    middle = flat_in + branch
    second_rms = inv_rms(middle)
    normed_mlp = (middle * second_rms * mlp_scale).astype(jnp.bfloat16)
    logits = jnp.dot(normed_mlp, router_all, preferred_element_type=jnp.float32)
    chances = jax.nn.softmax(logits, axis=-1)
    routed = routes.reshape(rows, TOPK)
    gates = jnp.take_along_axis(chances, routed, axis=-1)
    slots, token_of, filled = slot_table(routed)
    dispatched = (normed_mlp[token_of] * filled[:, None].astype(jnp.bfloat16)).reshape(
        EXPERTS, CAP, width
    )
    gate_up_all, down_all = (
        lax.all_gather(gate_up_weight, ("fsdp", "ctx"), axis=0, tiled=True),
        lax.all_gather(down_weight, ("fsdp", "ctx"), axis=0, tiled=True),
    )
    gate_up = jnp.einsum(
        "ecd,djef->ecjf", dispatched, gate_up_all, preferred_element_type=jnp.float32
    )
    gate_part = gate_up[:, :, 0]
    up_part = gate_up[:, :, 1]
    activated = (jax.nn.silu(gate_part) * up_part).astype(jnp.bfloat16)
    upstream = cotangent.reshape(rows, width).astype(jnp.float32)
    slot_gates = (
        jnp.zeros((EXPERTS * CAP,), jnp.float32)
        .at[slots.reshape(-1)]
        .set(gates.reshape(-1))
        .reshape(EXPERTS, CAP)
    )
    token_grid = token_of.reshape(EXPERTS, CAP)
    filled_grid = filled.reshape(EXPERTS, CAP)

    def expert_forward(expert_index, running):
        combined, slot_products = running
        expert_down = lax.dynamic_index_in_dim(down_all, expert_index, 1, keepdims=False)
        expert_act = lax.dynamic_index_in_dim(activated, expert_index, 0, keepdims=False)
        expert_tokens = lax.dynamic_index_in_dim(token_grid, expert_index, 0, keepdims=False)
        expert_gates = lax.dynamic_index_in_dim(slot_gates, expert_index, 0, keepdims=False)
        returned_rows = jnp.einsum(
            "cf,df->cd", expert_act, expert_down, preferred_element_type=jnp.float32
        )
        combined = combined.at[expert_tokens].add(returned_rows * expert_gates[:, None])
        products = jnp.sum(returned_rows * upstream[expert_tokens], axis=-1)
        slot_products = lax.dynamic_update_index_in_dim(slot_products, products, expert_index, 0)
        return (combined, slot_products)

    combined, slot_products = lax.fori_loop(
        0,
        EXPERTS,
        expert_forward,
        (jnp.zeros((rows, width), jnp.float32), jnp.zeros((EXPERTS, CAP), jnp.float32)),
    )
    gate_grad_part = slot_products.reshape(-1)[slots]
    expert_sum = lax.psum(combined, "tp")
    output = (middle + expert_sum).astype(jnp.bfloat16).reshape(seq_dev, block, width)
    slot_grads = (
        (slot_gates.reshape(-1)[:, None] * upstream[token_of])
        .astype(jnp.bfloat16)
        .reshape(EXPERTS, CAP, width)
    )
    gate_up_back, down_back = (
        lax.all_gather(gate_up_weight, ("fsdp", "ctx"), axis=0, tiled=True),
        lax.all_gather(down_weight, ("fsdp", "ctx"), axis=0, tiled=True),
    )
    act_grads = jnp.einsum(
        "ecd,def->ecf", slot_grads, down_back, preferred_element_type=jnp.float32
    )
    sigmoid = jax.nn.sigmoid(gate_part)
    gate_grads = act_grads * up_part * sigmoid * (1.0 + gate_part * (1.0 - sigmoid))
    up_grads = act_grads * (gate_part * sigmoid)
    pre_grads = jnp.stack([gate_grads, up_grads], axis=2).astype(jnp.bfloat16)

    def expert_backward(expert_index, running):
        expert_pre = lax.dynamic_index_in_dim(pre_grads, expert_index, 0, keepdims=False)
        expert_weight = lax.dynamic_index_in_dim(gate_up_back, expert_index, 2, keepdims=False)
        expert_tokens = lax.dynamic_index_in_dim(token_grid, expert_index, 0, keepdims=False)
        expert_filled = lax.dynamic_index_in_dim(filled_grid, expert_index, 0, keepdims=False)
        expert_back = jnp.einsum(
            "cjf,djf->cd", expert_pre, expert_weight, preferred_element_type=jnp.float32
        )
        return running.at[expert_tokens].add(expert_back * expert_filled[:, None])

    expert_input_part = lax.fori_loop(
        0, EXPERTS, expert_backward, jnp.zeros((rows, width), jnp.float32)
    )
    gate_up_term = jnp.einsum(
        "ecd,ecjf->djef", dispatched, pre_grads, preferred_element_type=jnp.float32
    )
    down_term = jnp.einsum(
        "ecf,ecd->def", activated, slot_grads, preferred_element_type=jnp.float32
    )
    expert_grads = lax.psum_scatter(
        jnp.concatenate([gate_up_term, down_term[:, None]], axis=1),
        ("fsdp", "ctx"),
        scatter_dimension=0,
        tiled=True,
    )
    gate_up_share = expert_grads[:, :2]
    down_share = expert_grads[:, 2]
    expert_input, gate_total = lax.psum((expert_input_part, gate_grad_part), "tp")
    chosen = (routed[:, :, None] == jnp.arange(EXPERTS, dtype=jnp.int32)[None, None, :]).astype(
        jnp.float32
    )
    chance_grads = jnp.sum(gate_total[:, :, None] * chosen, axis=1)
    logit_grads = chances * (chance_grads - jnp.sum(chances * chance_grads, axis=-1, keepdims=True))
    router_f32 = router_all.astype(jnp.float32)
    mlp_input = expert_input + jnp.dot(logit_grads, router_f32.T, precision=highest)
    grad_router = jnp.dot(normed_mlp.astype(jnp.float32).T, logit_grads, precision=highest)
    grad_mlp_gain = jnp.sum(mlp_input * middle * second_rms, axis=0)
    scaled_mlp = mlp_input * mlp_scale
    middle_grad = (
        upstream
        + second_rms * scaled_mlp
        - middle * second_rms**3 / width * jnp.sum(scaled_mlp * middle, axis=-1, keepdims=True)
    )
    branch_grad = middle_grad.astype(jnp.bfloat16)
    grad_out = jnp.einsum("td,th->dh", branch_grad, attended, preferred_element_type=jnp.float32)
    attended_grad = (
        jnp.dot(branch_grad, out_all, preferred_element_type=jnp.float32)
        .astype(jnp.bfloat16)
        .reshape(head_shape)
    )
    again_scores = (
        jnp.einsum("sqhd,skhd->shqk", query_rot, key_all, preferred_element_type=jnp.float32)
        * scale
    )
    again_scores = jnp.where(allowed, again_scores, -1e30)
    recomputed = jnp.exp(again_scores - log_total)
    prob_grads = jnp.einsum(
        "sqhd,skhd->shqk", attended_grad, value_all, preferred_element_type=jnp.float32
    )
    score_grads = (
        recomputed * (prob_grads - jnp.sum(recomputed * prob_grads, axis=-1, keepdims=True))
    ).astype(jnp.bfloat16)
    query_grads = (
        jnp.einsum("shqk,skhd->sqhd", score_grads, key_all, preferred_element_type=jnp.float32)
        * scale
    )
    key_grads = (
        jnp.einsum("shqk,sqhd->skhd", score_grads, query_rot, preferred_element_type=jnp.float32)
        * scale
    )
    value_grads = jnp.einsum(
        "shqk,sqhd->skhd",
        recomputed.astype(jnp.bfloat16),
        attended_grad,
        preferred_element_type=jnp.float32,
    )
    key_back, value_back = (
        lax.psum_scatter(key_grads, "ctx", scatter_dimension=1, tiled=True),
        lax.psum_scatter(value_grads, "ctx", scatter_dimension=1, tiled=True),
    )
    query_norm_grad = rotate_back(query_grads, cos_heads, sin_heads).reshape(rows, -1)
    key_norm_grad = rotate_back(key_back, cos_heads, sin_heads).reshape(rows, -1)
    query_scaled = query_norm_grad * query_gain
    key_scaled = key_norm_grad * key_gain
    query_inner, key_inner = lax.psum(
        (jnp.sum(query_scaled * query_proj, axis=-1), jnp.sum(key_scaled * key_proj, axis=-1)), "tp"
    )
    query_pre = query_rms * query_scaled - query_proj * query_rms**3 / HQ * query_inner[:, None]
    key_pre = key_rms * key_scaled - key_proj * key_rms**3 / HQ * key_inner[:, None]
    gain_terms = jnp.stack(
        [
            jnp.sum(query_norm_grad * query_proj * query_rms, axis=0),
            jnp.sum(key_norm_grad * key_proj * key_rms, axis=0),
        ]
    )
    grad_qk_gains = lax.psum(gain_terms, ("fsdp", "ctx"))
    proj_grads = jnp.stack([query_pre, key_pre, value_back.reshape(rows, -1)], axis=1).astype(
        jnp.bfloat16
    )
    grad_qkv = jnp.einsum("td,tch->dch", normed, proj_grads, preferred_element_type=jnp.float32)
    normed_grad = lax.psum(
        jnp.einsum("tch,dch->td", proj_grads, qkv_all, preferred_element_type=jnp.float32), "tp"
    )
    grad_attn_gain = jnp.sum(normed_grad * flat_in * first_rms, axis=0)
    scaled_first = normed_grad * attn_scale
    grad_inputs = (
        middle_grad
        + first_rms * scaled_first
        - flat_in * first_rms**3 / width * jnp.sum(scaled_first * flat_in, axis=-1, keepdims=True)
    )
    shares = (
        lax.psum_scatter(grad_attn_gain, ("fsdp", "ctx"), scatter_dimension=0, tiled=True),
        lax.psum_scatter(grad_qkv, ("fsdp", "ctx"), scatter_dimension=0, tiled=True),
        lax.psum_scatter(grad_out, ("fsdp", "ctx"), scatter_dimension=0, tiled=True),
        lax.psum_scatter(grad_mlp_gain, ("fsdp", "ctx"), scatter_dimension=0, tiled=True),
        lax.psum_scatter(grad_router, ("fsdp", "ctx"), scatter_dimension=0, tiled=True),
    )
    return (
        output,
        grad_inputs.reshape(seq_dev, block, width),
        shares[0],
        shares[1],
        shares[2],
        grad_qk_gains,
        shares[3],
        shares[4],
        gate_up_share,
        down_share,
    )


def solution(mesh):
    placed = (
        P("fsdp", "ctx", None),
        P(("fsdp", "ctx")),
        P(("fsdp", "ctx"), None, "tp"),
        P(("fsdp", "ctx"), "tp"),
        P(None, "tp"),
        P(("fsdp", "ctx")),
        P(("fsdp", "ctx"), None),
        P(("fsdp", "ctx"), None, None, "tp"),
        P(("fsdp", "ctx"), None, "tp"),
        P("ctx", "fsdp", None, None),
        P("fsdp", "ctx", None),
    )
    return jax.shard_map(
        on_device,
        mesh=mesh,
        in_specs=placed,
        out_specs=(
            P("fsdp", "ctx", None),
            P("fsdp", "ctx", None),
            P(("fsdp", "ctx")),
            P(("fsdp", "ctx"), None, "tp"),
            P(("fsdp", "ctx"), "tp"),
            P(None, "tp"),
            P(("fsdp", "ctx")),
            P(("fsdp", "ctx"), None),
            P(("fsdp", "ctx"), None, None, "tp"),
            P(("fsdp", "ctx"), None, "tp"),
        ),
        check_vma=False,
    )
```

profile of v0, /device:TPU:0, one launch (start us, length us, event | category | flops | bytes accessed | tf_op | source)
XLA Modules:
  0.0 2206.6 jit_solution(5604651613465843333)
XLA Ops:
  8.6 22.6 %all-gather = bf16[8,1,256]{2,1,0:T(2,128)(2,1)S(1)} all-gather(bf16[1,1,256]{2,1,0:T(2,128)(2,1)S(1)} %reshape.832), channel_id=1, replica_groups=mesh['fsdp'=2,'ctx'=4,'tp'=4] {'fsdp','ctx'}, dimensions={0}, use_global_device_ids=true | all-gather | bytes 4608 | tf_op jit(solution)/shard_map/all_gather | solution.py:78
  33.5 78.4 %all-gather.9.cloned.1.call-done = bf16[2048,3,512]{2,0,1:T(8,128)(2,1)} async-done(((bf16[256,3,512]{2,0,1:T(8,128)(2,1)}), bf16[2048,3,512]{2,0,1:T(8,128)(2,1)}) %all-gather.9.cloned.1.call-update) | async-done | bytes 6291472 | tf_op jit(solution)/shard_map/all_gather | solution.py:79
  118.0 6.0 all-reduce.4
  131.8 21.5 all-gather.13.cloned.1.call-done
  158.5 26.7 %all-gather.11.cloned.1.call-done = bf16[1,1024,4,128]{1,3,2,0:T(8,128)(2,1)} async-done(((bf16[1,256,4,128]{1,3,2,0:T(8,128)(2,1)}), bf16[1,1024,4,128]{1,3,2,0:T(8,128)(2,1)}) %all-gather.11.cloned.1.call-update) | async-done | bytes 1048592 | tf_op jit(solution)/shard_map/all_gather | solution.py:110
  188.7 46.1 %all-gather.15.cloned.1.call-done = bf16[2048,512]{1,0:T(8,128)(2,1)} async-done(((bf16[256,512]{1,0:T(8,128)(2,1)}), bf16[2048,512]{1,0:T(8,128)(2,1)}) %all-gather.15.cloned.1.call-update) | async-done | bytes 2097168 | tf_op jit(solution)/shard_map/all_gather | solution.py:80
  252.7 18.0 all-gather.1
  277.3 7.2 gather_fusion.2
  284.5 30.8 %all_gather.37 = bf16[2048,8]{0,1:T(8,128)(2,1)S(1)} all-gather(bf16[256,8]{0,1:T(8,128)(2,1)S(1)} %copy-done.73), channel_id=1, replica_groups=mesh['fsdp'=2,'ctx'=4,'tp'=4] {'fsdp','ctx'}, dimensions={0}, use_global_device_ids=true | all-gather | bytes 36864 | tf_op jit(solution)/shard_map/all_gather | solution.py:82
  319.5 6.1 gather_fusion.1
  326.1 6.5 gather_fusion.4
  337.1 182.0 %all-gather.17.cloned.1.call-done = bf16[2048,2,8,256]{3,0,1,2:T(8,128)(2,1)} async-done(((bf16[256,2,8,256]{3,0,1,2:T(8,128)(2,1)}), bf16[2048,2,8,256]{3,0,1,2:T(8,128)(2,1)}) %all-gather.17.cloned.1.call-update) | async-done | bytes 16777232 | tf_op jit(solution)/shard_map/all_gather | solution.py:147
  519.1 11.7 fusion.16
  530.8 114.3 %all-gather.19.cloned.1.call-done = bf16[2048,8,256]{2,0,1:T(8,128)(2,1)} async-done(((bf16[256,8,256]{2,0,1:T(8,128)(2,1)}), bf16[2048,8,256]{2,0,1:T(8,128)(2,1)}) %all-gather.19.cloned.1.call-update) | async-done | bytes 8388624 | tf_op jit(solution)/shard_map/all_gather | solution.py:148
  645.2 10.0 fusion.51
  658.3 63.9 %while.29 = (s32[]{:T(128)}, f32[256,2048]{1,0:T(8,128)}, s32[8,160]{1,0:T(8,128)S(1)}, bf16[8,160,2,256]{3,1,2,0:T(8,128)(2,1)}, bf16[2048,2,8,256]{3,0,1,2:T(8,128)(2,1)}, /*index=5*/f32[8,160]{1,0:T(8,128)S(1)}, s32[]{:T(128)}) while((s32[]{:T(128)}, f32[256,2048]{1,0:T(8,128)}, s32[8,160]{1,0:T(8,128)S(1)}, ...), condition=%wide.region_24.25_spmd, body=%wide.region_22.24_spmd.sunk | while | flops 336200160 | bytes 7508829 | solution.py:216
  723.8 80.3 %while.28 = (s32[]{:T(128)}, f32[256,2048]{1,0:T(8,128)}, f32[8,160]{1,0:T(8,128)S(1)}, s32[8,160]{1,0:T(8,128)S(1)}, bf16[8,160,256]{2,1,0:T(8,128)(2,1)}, /*in...) while((s32[]{:T(128)}, f32[256,2048]{1,0:T(8,128)}, ...), condition=%wide.region_20.21_spmd, body=%wide.region_17.20_spmd.sunk | while | flops 169084224 | bytes 9793273 | solution.py:180
  804.2 6.2 gather_fusion.3
  810.5 25.5 %psum.75 = f32[256,4]{1,0:T(8,128)S(1)} all-reduce(f32[256,4]{1,0:T(8,128)S(1)} %reshape.775), channel_id=1, replica_groups=mesh['fsdp'=2,'ctx'=4,'tp'=4] {'tp'}, use_global_device_ids=true, to_apply=%region_26.27 | all-reduce | flops 1024 | bytes 8192 | tf_op jit(solution)/shard_map/psum | solution.py:233
  856.5 18.8 convolution_bitcast_fusion.1
  878.6 9.9 reduce-scatter.9.cloned.1.call-done
  890.5 43.5 %reduce-scatter.7.cloned.1.call-done = f32[1,256,4,128]{3,1,2,0:T(8,128)} async-done(((f32[1,1024,4,128]{3,1,2,0:T(8,128)}), f32[1,256,4,128]{3,1,2,0:T(8,128)}) %reduce-scatter.7.cloned.1.call-update) | async-done | bytes 524304 | tf_op jit(solution)/shard_map/reduce_scatter | solution.py:283
  938.5 6.5 all-reduce.3
  954.0 12.9 convolution_bitcast_fusion.2
  966.9 33.6 %pad_maximum_fusion = f32[2048,3,8,256]{0,3,1,2:T(8,128)} fusion(f32[2048,1,8,256]{0,3,1,2:T(8,128)} %convolution_bitcast_fusion.2, f32[2048,2,8,256]{0,3,1,2:T(8,128)} %convolution_bitcast_fusion.1), kind=kLoop, calls=%fused_computation.32 | loop fusion | flops 12582912 | bytes 100663296 | tf_op jit(solution)/shard_map/concatenate | solution.py:226
  1008.9 7.4 fusion.64
  1018.2 19.5 all-reduce.14.cloned.1.call-done
  1039.8 38.9 %all-reduce.2 = (f32[2048]{0:T(1024)S(1)}, f32[2,512]{1,0:T(2,128)}, f32[2048]{0:T(1024)S(1)}) all-reduce(f32[2048]{0:T(1024)S(1)} %get-tuple-element.336, f32[2,512]{1,0:T(2,128)S(1)} %pad_maximum_fusion.6, f32[2048]{0:T(1024)S(1)} %get-tuple-element.334), channel_id=4, replica_groups=mesh['fsdp'=2,'ctx'=4,'tp'=4] {'fsdp','ctx'}, use_global_device_ids=true, to_apply=%region_40.41.clone | all-reduce | flops 5120 | bytes 40960
  1085.0 747.3 %reduce-scatter.17.cloned.1.call-done = f32[256,3,8,256]{0,3,1,2:T(8,128)} async-done(((f32[2048,3,8,256]{0,3,1,2:T(8,128)}), f32[256,3,8,256]{0,3,1,2:T(8,128)}) %reduce-scatter.17.cloned.1.call-update) | async-done | bytes 6291472 | tf_op jit(solution)/shard_map/reduce_scatter | solution.py:225
  1846.1 50.5 %reduce-scatter.15.cloned.1.call-done = f32[256,8]{0,1:T(8,128)} async-done(((f32[2048,8]{0,1:T(8,128)}), f32[256,8]{0,1:T(8,128)}) %reduce-scatter.15.cloned.1.call-update) | async-done | bytes 8208 | tf_op jit(solution)/shard_map/reduce_scatter | solution.py:321
  1896.6 91.0 %reduce-scatter.13.cloned.1.call-done = f32[256,512]{1,0:T(8,128)} async-done(((f32[2048,512]{1,0:T(8,128)}), f32[256,512]{1,0:T(8,128)}) %reduce-scatter.13.cloned.1.call-update) | async-done | bytes 524304 | tf_op jit(solution)/shard_map/reduce_scatter | solution.py:319
  1987.7 212.1 %reduce-scatter.11.cloned.1.call-done = f32[256,3,512]{2,0,1:T(8,128)} async-done(((f32[2048,3,512]{2,0,1:T(8,128)}), f32[256,3,512]{2,0,1:T(8,128)}) %reduce-scatter.11.cloned.1.call-update) | async-done | bytes 1572880 | tf_op jit(solution)/shard_map/reduce_scatter | solution.py:318
  (397 shorter events, 278.7 us)
Async XLA Ops:
  7.2 104.8 %all-gather.9.cloned.1.call-start = ((), (), s32[]{:S(2)}) async-start(), calls=%async_computation.6 | async-start | bytes 7077888 | tf_op jit(solution)/shard_map/all_gather | solution.py:79
  7.9 145.3 %all-gather.13.cloned.1.call-start = ((), (), s32[]{:S(2)}) async-start(), calls=%async_computation.8 | async-start | bytes 1310720 | tf_op jit(solution)/shard_map/all_gather | solution.py:109
  31.2 85.3 %copy-start.43 = (f32[8,1,256]{2,1,0:T(1,128)}, f32[8,1,256]{2,1,0:T(1,128)S(1)}, u32[]{:S(2)}) copy-start(f32[8,1,256]{2,1,0:T(1,128)S(1)} %convert_element_type.162) | copy-start | bytes 24580
  32.7 97.7 %copy-start.28 = (f32[256,128]{1,0:T(8,128)}, f32[256,128]{1,0:T(8,128)S(1)}, u32[]{:S(2)}) copy-start(f32[256,128]{1,0:T(8,128)S(1)} %get-tuple-element.404) | copy-start | bytes 393220
  32.7 97.8 %copy-start.26 = (f32[256,128]{1,0:T(8,128)}, f32[256,128]{1,0:T(8,128)S(1)}, u32[]{:S(2)}) copy-start(f32[256,128]{1,0:T(8,128)S(1)} %get-tuple-element.405) | copy-start | bytes 393220
  33.5 83.1 %copy-start.60 = (f32[256]{0:T(256)}, f32[256]{0:T(256)S(1)}, u32[]{:S(2)}) copy-start(f32[256]{0:T(256)S(1)} %get-tuple-element.411) | copy-start | bytes 3076
  33.5 92.6 %copy-start.50 = (f32[1,512]{1,0:T(1,128)}, f32[1,512]{1,0:T(1,128)S(1)}, u32[]{:S(2)}) copy-start(f32[1,512]{1,0:T(1,128)S(1)} %get-tuple-element.408) | copy-start | bytes 6148
  33.5 98.1 %copy-start.52 = (f32[1,512]{1,0:T(1,128)}, f32[1,512]{1,0:T(1,128)S(1)}, u32[]{:S(2)}) copy-start(f32[1,512]{1,0:T(1,128)S(1)} %get-tuple-element.409) | copy-start | bytes 6148
  127.1 58.0 %all-gather.11.cloned.1.call-start = ((), (), s32[]{:S(2)}) async-start(), calls=%async_computation.7 | async-start | bytes 1310720 | tf_op jit(solution)/shard_map/all_gather | solution.py:110
  129.7 105.0 %all-gather.15.cloned.1.call-start = ((), (), s32[]{:S(2)}) async-start(), calls=%async_computation.9 | async-start | bytes 2359296 | tf_op jit(solution)/shard_map/all_gather | solution.py:80
  130.3 185.7 %all-reduce.10.cloned.1.call-start = ((), (), s32[]{:S(2)}) async-start(), calls=%async_computation.10 | async-start | bytes 4194304 | tf_op jit(solution)/shard_map/psum | solution.py:132
  188.7 46.1 %copy-start.37 = (bf16[4,128,256]{2,1,0:T(8,128)(2,1)}, bf16[4,128,256]{2,1,0:T(8,128)(2,1)S(1)}, u32[]{:S(2)}) copy-start(bf16[4,128,256]{2,1,0:T(8,128)(2,1)S(1)} %fusion.42) | copy-start | bytes 786436
  238.5 280.7 %all-gather.17.cloned.1.call-start = ((), (), s32[]{:S(2)}) async-start(), calls=%async_computation.11 | async-start | bytes 18874368 | tf_op jit(solution)/shard_map/all_gather | solution.py:147
  242.1 403.1 %all-gather.19.cloned.1.call-start = ((), (), s32[]{:S(2)}) async-start(), calls=%async_computation.12 | async-start | bytes 9437184 | tf_op jit(solution)/shard_map/all_gather | solution.py:148
  244.6 591.7 %all-reduce.12.cloned.1.call-start = ((), (), s32[]{:S(2)}) async-start(), calls=%async_computation.13 | async-start | bytes 4194304 | tf_op jit(solution)/shard_map/psum | solution.py:233
  270.7 47.9 %copy-start.45 = (f32[8,1,256]{2,1,0:T(1,128)}, f32[8,1,256]{2,1,0:T(1,128)S(1)}, u32[]{:S(2)}) copy-start(f32[8,1,256]{2,1,0:T(1,128)S(1)} %convert_element_type.163) | copy-start | bytes 24580
  722.2 166.4 %reduce-scatter.9.cloned.1.call-start = ((), (), s32[]{:S(2)}) async-start(), calls=%async_computation.15 | async-start | bytes 2621440 | tf_op jit(solution)/shard_map/reduce_scatter | solution.py:284
  804.2 32.0 %copy-start.67 = (f32[256]{0:T(256)S(1)}, f32[256]{0:T(256)}, u32[]{:S(2)}) copy-start(f32[256]{0:T(256)} %copy-done.66) | copy-start | bytes 3076
  804.2 32.1 %copy-start.5 = (f32[256,2048]{1,0:T(8,128)S(1)}, f32[256,2048]{1,0:T(8,128)}, u32[]{:S(2)}) copy-start(f32[256,2048]{1,0:T(8,128)} %copy-done.4) | copy-start | bytes 6291460
  804.2 32.1 %copy-start.42 = (bf16[2048,8]{0,1:T(8,128)(2,1)S(1)}, bf16[2048,8]{0,1:T(8,128)(2,1)}, u32[]{:S(2)}) copy-start(bf16[2048,8]{0,1:T(8,128)(2,1)} %copy-done.41) | copy-start | bytes 98308
  804.2 32.1 %copy-start.46 = (f32[8,1,256]{2,1,0:T(1,128)S(1)}, f32[8,1,256]{2,1,0:T(1,128)}, u32[]{:S(2)}) copy-start(f32[8,1,256]{2,1,0:T(1,128)} %copy-done.45) | copy-start | bytes 24580
  804.2 32.1 %copy-start.63 = (f32[256]{0:T(256)S(1)}, f32[256]{0:T(256)}, u32[]{:S(2)}) copy-start(f32[256]{0:T(256)} %copy-done.62) | copy-start | bytes 3076
  846.9 87.2 %reduce-scatter.7.cloned.1.call-start = ((), (), s32[]{:S(2)}) async-start(), calls=%async_computation.14 | async-start | bytes 2621440 | tf_op jit(solution)/shard_map/reduce_scatter | solution.py:283
  855.3 182.4 %all-reduce.14.cloned.1.call-start = ((), (), s32[]{:S(2)}) async-start(), calls=%async_computation.20 | async-start | bytes 8388608 | tf_op jit(solution)/shard_map/psum | solution.py:187
  876.6 57.4 %copy-start.29 = (f32[256,128]{1,0:T(8,128)S(1)}, f32[256,128]{1,0:T(8,128)}, u32[]{:S(2)}) copy-start(f32[256,128]{1,0:T(8,128)} %copy-done.28) | copy-start | bytes 393220
  889.6 45.8 %copy-start.18 = (f32[1,256,4,128]{3,2,1,0:T(4,128)S(1)}, f32[1,256,4,128]{3,2,1,0:T(4,128)}, u32[]{:S(2)}) copy-start(f32[1,256,4,128]{3,2,1,0:T(4,128)} %copy-done.17) | copy-start | bytes 1572868
  889.6 45.8 %copy-start.27 = (f32[256,128]{1,0:T(8,128)S(1)}, f32[256,128]{1,0:T(8,128)}, u32[]{:S(2)}) copy-start(f32[256,128]{1,0:T(8,128)} %copy-done.26) | copy-start | bytes 393220
  889.6 45.8 %copy-start.57 = (f32[256]{0:T(256)S(1)}, f32[256]{0:T(256)}, u32[]{:S(2)}) copy-start(f32[256]{0:T(256)} %copy-done.56) | copy-start | bytes 3076
  953.0 879.3 %reduce-scatter.17.cloned.1.call-start = ((), (), s32[]{:S(2)}) async-start(), calls=%async_computation.19 | async-start | bytes 56623104 | tf_op jit(solution)/shard_map/reduce_scatter | solution.py:225
  1000.6 896.1 %reduce-scatter.15.cloned.1.call-start = ((), (), s32[]{:S(2)}) async-start(), calls=%async_computation.18 | async-start | bytes 73728 | tf_op jit(solution)/shard_map/reduce_scatter | solution.py:321
  1003.1 984.6 %reduce-scatter.13.cloned.1.call-start = ((), (), s32[]{:S(2)}) async-start(), calls=%async_computation.17 | async-start | bytes 4718592 | tf_op jit(solution)/shard_map/reduce_scatter | solution.py:319
  1007.7 1192.1 %reduce-scatter.11.cloned.1.call-start = ((), (), s32[]{:S(2)}) async-start(), calls=%async_computation.16 | async-start | bytes 14155776 | tf_op jit(solution)/shard_map/reduce_scatter | solution.py:318
  (59 other events, 426.4 us)
Sparse Core Ops, SparseCore 0:
  10.2 101.7 all-gather.8
  127.2 25.9 all-gather.12
  155.4 29.6 all-gather.10
  187.1 47.5 all-gather.14
  238.6 49.8 all-reduce.9
  291.3 227.7 all-gather.16
  522.0 123.1 all-gather.18
  722.3 49.5 all-reduce.11
  847.0 41.5 reduce-scatter.8
  890.8 43.1 reduce-scatter.6
  953.1 84.5 all-reduce.13
  1041.9 790.2 reduce-scatter.16
  1836.2 60.3 reduce-scatter.14
  1900.7 86.9 reduce-scatter.12
  1992.1 207.5 reduce-scatter.10
where the time goes:
time: 2220 us; the launch traced here: 2210 us
  waiting for transfers between devices  1640 us (74%)
  other arithmetic  150 us (7%)
  blocking collectives  148 us (7%)
  matrix products  141 us (6%)
  local copies, waits for them, and re-layouts  106 us (5%)
    reduce_scatter x1, waiting for transfers between devices, on_device(): lax.psum_scatter(jnp.concatenate([gate_up_term, down_term[:, None]], axis...  747 us
    reduce_scatter x1, waiting for transfers between devices, on_device(): lax.psum_scatter(grad_qkv, ('fsdp', 'ctx'), scatter_dimension=0, tiled=True)  212 us
    all_gather x1, waiting for transfers between devices, on_device(): lax.all_gather(gate_up_weight, ('fsdp', 'ctx'), axis=0, tiled=True)  182 us
    all_gather x1, waiting for transfers between devices, on_device(): lax.all_gather(down_weight, ('fsdp', 'ctx'), axis=0, tiled=True)  114 us
    reduce_scatter x1, waiting for transfers between devices, on_device(): lax.psum_scatter(grad_out, ('fsdp', 'ctx'), scatter_dimension=0, tiled=True)  91 us
    all_gather x1, waiting for transfers between devices, on_device(): lax.all_gather(qkv_weight, ('fsdp', 'ctx'), axis=0, tiled=True)  78.4 us
    reduce_scatter x1, waiting for transfers between devices, on_device(): lax.psum_scatter(grad_router, ('fsdp', 'ctx'), scatter_dimension=0, tiled...  50.5 us
    all_gather x1, waiting for transfers between devices, on_device(): lax.all_gather(out_weight, ('fsdp', 'ctx'), axis=0, tiled=True)  46.1 us
  transfers between devices with their start and end apart: 15, of which 13 were waited for; matrix products, arithmetic and copies ran while one was open for 12% of the time, Pallas kernels for 0%

commit v1 on v0

--- a/solution.py
+++ b/solution.py
@@ -11,6 +11,19 @@
 CAP = 160
 epsilon = 1e-05
 highest = lax.Precision.HIGHEST
+
+
+def ring_gather(x, axis, dim):
+    ways = lax.axis_size(axis)
+    up = [(d, (d + 1) % ways) for d in range(ways)]
+    down = [(d, (d - 1) % ways) for d in range(ways)]
+    earlier, later = ([x], [x])
+    for _ in range(ways // 2):
+        earlier.append(lax.ppermute(earlier[-1], axis, up))
+    for _ in range((ways - 1) // 2):
+        later.append(lax.ppermute(later[-1], axis, down))
+    line = jnp.concatenate([*earlier[::-1], *later[1:]], axis=dim)
+    return jnp.roll(line, (lax.axis_index(axis) - ways // 2) * x.shape[dim], axis=dim)
 
 
 def inv_rms(values):
@@ -77,7 +90,7 @@
     attn_gain_all, qkv_all, out_all, mlp_gain_all, router_all = (
         lax.all_gather(attn_gain, ("fsdp", "ctx"), axis=0, tiled=True),
         lax.all_gather(qkv_weight, ("fsdp", "ctx"), axis=0, tiled=True),
-        lax.all_gather(out_weight, ("fsdp", "ctx"), axis=0, tiled=True),
+        ring_gather(out_weight, ("fsdp", "ctx"), 0),
         lax.all_gather(mlp_gain, ("fsdp", "ctx"), axis=0, tiled=True),
         lax.all_gather(router_weight, ("fsdp", "ctx"), axis=0, tiled=True),
     )

time: 2220 us -> 2200 us (level)
  waiting for transfers between devices: 1640 us -> 1580 us
    all_gather x1 -> x0, waiting for transfers between devices: 46.1 us -> none  [on_device(): lax.all_gather(out_weight, ('fsdp', 'ctx'), axis=0, tiled=True)]
    all_gather x1, waiting for transfers between devices: 78.4 us -> 41.3 us  [on_device(): lax.all_gather(qkv_weight, ('fsdp', 'ctx'), axis=0, tiled=True)]
    ppermute x0 -> x7, waiting for transfers between devices: none -> 33.4 us  [the longest x4 33.4 us: ring_gather(): earlier.append(lax.ppermute(earlier[-1], axis, up))]
    unnamed x162 -> x203, local copies, waits for them, and re-layouts: 26.7 us -> 44.5 us
  transfers between devices with their start and end apart: 15 -> 21, of which waited for: 13 -> 15; matrix products, arithmetic and copies ran while one was open for 12% -> 14% of each run, Pallas kernels for 0% -> 0%
where the time goes in v1:
time: 2200 us; the launch traced here: 2190 us
  waiting for transfers between devices  1580 us (72%)
  other arithmetic  152 us (7%)
  blocking collectives  148 us (7%)
  matrix products  143 us (6%)
  local copies, waits for them, and re-layouts  124 us (6%)
  starting transfers between devices  22.5 us (1%)
    reduce_scatter x1, waiting for transfers between devices, on_device(): lax.psum_scatter(jnp.concatenate([gate_up_term, down_term[:, None]], axis...  749 us
    reduce_scatter x1, waiting for transfers between devices, on_device(): lax.psum_scatter(grad_qkv, ('fsdp', 'ctx'), scatter_dimension=0, tiled=True)  212 us
    all_gather x1, waiting for transfers between devices, on_device(): lax.all_gather(gate_up_weight, ('fsdp', 'ctx'), axis=0, tiled=True)  181 us
    all_gather x1, waiting for transfers between devices, on_device(): lax.all_gather(down_weight, ('fsdp', 'ctx'), axis=0, tiled=True)  114 us
    reduce_scatter x1, waiting for transfers between devices, on_device(): lax.psum_scatter(grad_out, ('fsdp', 'ctx'), scatter_dimension=0, tiled=True)  91.2 us
    reduce_scatter x1, waiting for transfers between devices, on_device(): lax.psum_scatter(grad_router, ('fsdp', 'ctx'), scatter_dimension=0, tiled...  50.4 us
    unnamed x203, local copies, waits for them, and re-layouts  44.5 us
    scatter-add x8, other arithmetic, expert_forward(): combined.at[expert_tokens].add(returned_rows * expert_gates[:, None])  44.4 us
  transfers between devices with their start and end apart: 21, of which 15 were waited for; matrix products, arithmetic and copies ran while one was open for 14% of the time, Pallas kernels for 0%

profile of v1, /device:TPU:0, one launch (start us, length us, event | category | flops | bytes accessed | tf_op | source)
XLA Modules:
  0.0 2186.8 jit_solution(3326291407101773893)
XLA Ops:
  21.5 16.7 collective-permute-done.1
  42.8 6.6 collective-permute-start.5
  49.4 10.9 collective-permute-done.2
  67.1 20.5 all-gather
  90.1 41.3 %all-gather.8.cloned.1.call-done = bf16[2048,3,512]{2,0,1:T(8,128)(2,1)} async-done(((bf16[256,3,512]{2,0,1:T(8,128)(2,1)}), bf16[2048,3,512]{2,0,1:T(8,128)(2,1)}) %all-gather.8.cloned.1.call-update) | async-done | bytes 6291472 | tf_op jit(solution)/shard_map/all_gather | solution.py:92
  137.5 6.8 all-reduce.4
  167.8 8.6 all-gather.12.cloned.1.call-done
  181.5 26.7 %all-gather.10.cloned.1.call-done = bf16[1,1024,4,128]{1,3,2,0:T(8,128)(2,1)} async-done(((bf16[1,256,4,128]{1,3,2,0:T(8,128)(2,1)}), bf16[1,1024,4,128]{1,3,2,0:T(8,128)(2,1)}) %all-gather.10.cloned.1.call-update) | async-done | bytes 1048592 | tf_op jit(solution)/shard_map/all_gather | solution.py:123
  230.6 18.8 all-gather.1
  255.7 7.1 gather_fusion.2
  262.8 30.9 %all_gather.33 = bf16[2048,8]{0,1:T(8,128)(2,1)S(1)} all-gather(bf16[256,8]{0,1:T(8,128)(2,1)S(1)} %copy-done.84), channel_id=1, replica_groups=mesh['fsdp'=2,'ctx'=4,'tp'=4] {'fsdp','ctx'}, dimensions={0}, use_global_device_ids=true | all-gather | bytes 36864 | tf_op jit(solution)/shard_map/all_gather | solution.py:95
  304.5 6.5 gather_fusion.4
  315.8 180.8 %all-gather.14.cloned.1.call-done = bf16[2048,2,8,256]{3,0,1,2:T(8,128)(2,1)} async-done(((bf16[256,2,8,256]{3,0,1,2:T(8,128)(2,1)}), bf16[2048,2,8,256]{3,0,1,2:T(8,128)(2,1)}) %all-gather.14.cloned.1.call-update) | async-done | bytes 16777232 | tf_op jit(solution)/shard_map/all_gather | solution.py:160
  496.6 11.8 fusion.16
  508.4 114.1 %all-gather.16.cloned.1.call-done = bf16[2048,8,256]{2,0,1:T(8,128)(2,1)} async-done(((bf16[256,8,256]{2,0,1:T(8,128)(2,1)}), bf16[2048,8,256]{2,0,1:T(8,128)(2,1)}) %all-gather.16.cloned.1.call-update) | async-done | bytes 8388624 | tf_op jit(solution)/shard_map/all_gather | solution.py:161
  622.5 10.0 fusion.58
  635.6 63.7 %while.29 = (s32[]{:T(128)}, f32[256,2048]{1,0:T(8,128)}, s32[8,160]{1,0:T(8,128)S(1)}, bf16[8,160,2,256]{3,1,2,0:T(8,128)(2,1)}, bf16[2048,2,8,256]{3,0,1,2:T(8,128)(2,1)}, /*index=5*/f32[8,160]{1,0:T(8,128)S(1)}, s32[]{:T(128)}) while((s32[]{:T(128)}, f32[256,2048]{1,0:T(8,128)}, s32[8,160]{1,0:T(8,128)S(1)}, ...), condition=%wide.region_24.25_spmd, body=%wide.region_22.24_spmd.sunk | while | flops 336200160 | bytes 7508829 | solution.py:229
  700.9 80.1 %while.28 = (s32[]{:T(128)}, f32[256,2048]{1,0:T(8,128)}, f32[8,160]{1,0:T(8,128)S(1)}, s32[8,160]{1,0:T(8,128)S(1)}, bf16[8,160,256]{2,1,0:T(8,128)(2,1)}, /*in...) while((s32[]{:T(128)}, f32[256,2048]{1,0:T(8,128)}, ...), condition=%wide.region_20.21_spmd, body=%wide.region_17.20_spmd.sunk | while | flops 169084224 | bytes 9793273 | solution.py:193
  787.5 25.6 %psum.75 = f32[256,4]{1,0:T(8,128)S(1)} all-reduce(f32[256,4]{1,0:T(8,128)S(1)} %reshape.775), channel_id=1, replica_groups=mesh['fsdp'=2,'ctx'=4,'tp'=4] {'tp'}, use_global_device_ids=true, to_apply=%region_26.27 | all-reduce | flops 1024 | bytes 8192 | tf_op jit(solution)/shard_map/psum | solution.py:246
  835.3 18.8 convolution_bitcast_fusion.1
  857.3 9.9 reduce-scatter.9.cloned.1.call-done
  869.2 43.7 %reduce-scatter.7.cloned.1.call-done = f32[1,256,4,128]{3,1,2,0:T(8,128)} async-done(((f32[1,1024,4,128]{3,1,2,0:T(8,128)}), f32[1,256,4,128]{3,1,2,0:T(8,128)}) %reduce-scatter.7.cloned.1.call-update) | async-done | bytes 524304 | tf_op jit(solution)/shard_map/reduce_scatter | solution.py:296
  917.4 6.6 all-reduce.3
  932.9 12.9 convolution_bitcast_fusion.2
  945.8 33.7 %pad_maximum_fusion = f32[2048,3,8,256]{0,3,1,2:T(8,128)} fusion(f32[2048,1,8,256]{0,3,1,2:T(8,128)} %convolution_bitcast_fusion.2, f32[2048,2,8,256]{0,3,1,2:T(8,128)} %convolution_bitcast_fusion.1), kind=kLoop, calls=%fused_computation.32 | loop fusion | flops 12582912 | bytes 100663296 | tf_op jit(solution)/shard_map/concatenate | solution.py:239
  987.9 7.5 fusion.71
  997.3 19.3 all-reduce.14.cloned.1.call-done
  1018.7 38.9 %all-reduce.2 = (f32[2048]{0:T(1024)S(1)}, f32[2,512]{1,0:T(2,128)}, f32[2048]{0:T(1024)S(1)}) all-reduce(f32[2048]{0:T(1024)S(1)} %get-tuple-element.336, f32[2,512]{1,0:T(2,128)S(1)} %pad_maximum_fusion.6, f32[2048]{0:T(1024)S(1)} %get-tuple-element.334), channel_id=4, replica_groups=mesh['fsdp'=2,'ctx'=4,'tp'=4] {'fsdp','ctx'}, use_global_device_ids=true, to_apply=%region_40.41.clone | all-reduce | flops 5120 | bytes 40960
  1063.9 748.7 %reduce-scatter.17.cloned.1.call-done = f32[256,3,8,256]{0,3,1,2:T(8,128)} async-done(((f32[2048,3,8,256]{0,3,1,2:T(8,128)}), f32[256,3,8,256]{0,3,1,2:T(8,128)}) %reduce-scatter.17.cloned.1.call-update) | async-done | bytes 6291472 | tf_op jit(solution)/shard_map/reduce_scatter | solution.py:238
  1826.4 50.4 %reduce-scatter.15.cloned.1.call-done = f32[256,8]{0,1:T(8,128)} async-done(((f32[2048,8]{0,1:T(8,128)}), f32[256,8]{0,1:T(8,128)}) %reduce-scatter.15.cloned.1.call-update) | async-done | bytes 8208 | tf_op jit(solution)/shard_map/reduce_scatter | solution.py:334
  1876.8 91.2 %reduce-scatter.13.cloned.1.call-done = f32[256,512]{1,0:T(8,128)} async-done(((f32[2048,512]{1,0:T(8,128)}), f32[256,512]{1,0:T(8,128)}) %reduce-scatter.13.cloned.1.call-update) | async-done | bytes 524304 | tf_op jit(solution)/shard_map/reduce_scatter | solution.py:332
  1968.0 212.0 %reduce-scatter.11.cloned.1.call-done = f32[256,3,512]{2,0,1:T(8,128)} async-done(((f32[2048,3,512]{2,0,1:T(8,128)}), f32[256,3,512]{2,0,1:T(8,128)}) %reduce-scatter.11.cloned.1.call-update) | async-done | bytes 1572880 | tf_op jit(solution)/shard_map/reduce_scatter | solution.py:331
  (450 shorter events, 333.4 us)
Async XLA Ops:
  7.2 124.3 %copy-start.8 = (bf16[1,256,2048]{2,1,0:T(8,128)(2,1)S(1)}, bf16[1,256,2048]{2,1,0:T(8,128)(2,1)}, u32[]{:S(2)}) copy-start(bf16[1,256,2048]{2,1,0:T(8,128)(2,1)} %param.15) | copy-start | bytes 3145732
  7.2 59.9 %copy-start.86 = (bf16[256]{0:T(256)(128)(2,1)S(1)}, bf16[256]{0:T(256)(128)(2,1)}, u32[]{:S(2)}) copy-start(bf16[256]{0:T(256)(128)(2,1)} %param.16) | copy-start | bytes 1540
  7.2 81.3 %copy-start.79 = (bf16[2,512]{1,0:T(2,128)(2,1)S(1)}, bf16[2,512]{1,0:T(2,128)(2,1)}, u32[]{:S(2)}) copy-start(bf16[2,512]{1,0:T(2,128)(2,1)} %param.19) | copy-start | bytes 6148
  7.2 124.2 %all-gather.8.cloned.1.call-start = ((), (), s32[]{:S(2)}) async-start(), calls=%async_computation.6 | async-start | bytes 7077888 | tf_op jit(solution)/shard_map/all_gather | solution.py:92
  7.9 168.4 %all-gather.12.cloned.1.call-start = ((), (), s32[]{:S(2)}) async-start(), calls=%async_computation.8 | async-start | bytes 1310720 | tf_op jit(solution)/shard_map/all_gather | solution.py:122
  8.0 13.4 collective-permute-start
  11.1 31.8 %collective-permute-start.4 = (bf16[256,512]{1,0:T(8,128)(2,1)}, bf16[256,512]{1,0:T(8,128)(2,1)S(1)}, u32[]{:S(2)}, u32[]{:S(2)}) collective-permute-start(bf16[256,512]{1,0:T(8,128)(2,1)} %param.18), channel_id=1, source_target_pairs={{0,28},{4,0},{8,4},{12,8},{16,12},{20,16},{24,20},{28,24},{1,29},{... | collective-permute-start | bytes 786440 | tf_op jit(solution)/shard_map/ppermute | solution.py:24
  21.4 110.0 %copy-start.41 = (bf16[256,512]{1,0:T(8,128)(2,1)}, bf16[256,512]{1,0:T(8,128)(2,1)S(1)}, u32[]{:S(2)}) copy-start(bf16[256,512]{1,0:T(8,128)(2,1)S(1)} %collective-permute-done) | copy-start | bytes 786436
  21.4 16.8 collective-permute-start.1
  38.2 93.2 %copy-start.43 = (bf16[256,512]{1,0:T(8,128)(2,1)}, bf16[256,512]{1,0:T(8,128)(2,1)S(1)}, u32[]{:S(2)}) copy-start(bf16[256,512]{1,0:T(8,128)(2,1)S(1)} %collective-permute-done.1) | copy-start | bytes 786436
  38.2 22.0 %collective-permute-start.2 = (bf16[256,512]{1,0:T(8,128)(2,1)S(1)}, bf16[256,512]{1,0:T(8,128)(2,1)S(1)}, u32[]{:S(2)}, u32[]{:S(2)}) collective-permute-start(bf16[256,512]{1,0:T(8,128)(2,1)S(1)} %collective-permute-done.1), channel_id=1, source_target_pairs={{0,4},{4,8},{8,12},{12,16},{16,20},{20,24},{24,28},{28,0},{1,5},{5... | collective-permute-start | bytes 786440 | tf_op jit(solution)/shard_map/ppermute | solution.py:22
  42.2 104.2 %copy-start.25 = (f32[256,128]{1,0:T(8,128)}, f32[256,128]{1,0:T(8,128)S(1)}, u32[]{:S(2)}) copy-start(f32[256,128]{1,0:T(8,128)S(1)} %get-tuple-element.405) | copy-start | bytes 393220
  42.2 104.2 %copy-start.27 = (f32[256,128]{1,0:T(8,128)}, f32[256,128]{1,0:T(8,128)S(1)}, u32[]{:S(2)}) copy-start(f32[256,128]{1,0:T(8,128)S(1)} %get-tuple-element.404) | copy-start | bytes 393220
  42.8 93.3 %copy-start.71 = (f32[256]{0:T(256)}, f32[256]{0:T(256)S(1)}, u32[]{:S(2)}) copy-start(f32[256]{0:T(256)S(1)} %get-tuple-element.411) | copy-start | bytes 3076
  42.8 88.6 %copy-start.39 = (bf16[256,512]{1,0:T(8,128)(2,1)}, bf16[256,512]{1,0:T(8,128)(2,1)S(1)}, u32[]{:S(2)}) copy-start(bf16[256,512]{1,0:T(8,128)(2,1)S(1)} %collective-permute-done.4) | copy-start | bytes 786436
  42.8 45.7 %collective-permute-start.5 = (bf16[256,512]{1,0:T(8,128)(2,1)S(1)}, bf16[256,512]{1,0:T(8,128)(2,1)}, u32[]{:S(2)}, u32[]{:S(2)}) collective-permute-start(bf16[256,512]{1,0:T(8,128)(2,1)S(1)} %collective-permute-done.4), channel_id=1, source_target_pairs={{0,28},{4,0},{8,4},{12,8},{16,12},{20,16},{24,20},{28,24},{1,29},{... | collective-permute-start | bytes 786440 | tf_op jit(solution)/shard_map/ppermute | solution.py:24
  60.3 71.2 %copy-start.45 = (bf16[256,512]{1,0:T(8,128)(2,1)}, bf16[256,512]{1,0:T(8,128)(2,1)S(1)}, u32[]{:S(2)}) copy-start(bf16[256,512]{1,0:T(8,128)(2,1)S(1)} %collective-permute-done.2) | copy-start | bytes 786436
  60.3 28.3 %collective-permute-start.3 = (bf16[256,512]{1,0:T(8,128)(2,1)S(1)}, bf16[256,512]{1,0:T(8,128)(2,1)S(1)}, u32[]{:S(2)}, u32[]{:S(2)}) collective-permute-start(bf16[256,512]{1,0:T(8,128)(2,1)S(1)} %collective-permute-done.2), channel_id=1, source_target_pairs={{0,4},{4,8},{8,12},{12,16},{16,20},{20,24},{24,28},{28,0},{1,5},{5... | collective-permute-start | bytes 786440 | tf_op jit(solution)/shard_map/ppermute | solution.py:22
  88.5 79.0 %copy-start.63 = (f32[1,512]{1,0:T(1,128)}, f32[1,512]{1,0:T(1,128)S(1)}, u32[]{:S(2)}) copy-start(f32[1,512]{1,0:T(1,128)S(1)} %get-tuple-element.409) | copy-start | bytes 6148
  88.5 67.7 %collective-permute-start.6 = (bf16[256,512]{1,0:T(8,128)(2,1)}, bf16[256,512]{1,0:T(8,128)(2,1)}, u32[]{:S(2)}, u32[]{:S(2)}) collective-permute-start(bf16[256,512]{1,0:T(8,128)(2,1)} %collective-permute-done.5), channel_id=1, source_target_pairs={{0,28},{4,0},{8,4},{12,8},{16,12},{20,16},{24,20},{28,24},{1,29},{... | collective-permute-start | bytes 786440 | tf_op jit(solution)/shard_map/ppermute | solution.py:24
  147.5 60.7 %all-gather.10.cloned.1.call-start = ((), (), s32[]{:S(2)}) async-start(), calls=%async_computation.7 | async-start | bytes 1310720 | tf_op jit(solution)/shard_map/all_gather | solution.py:123
  166.7 127.6 %all-reduce.10.cloned.1.call-start = ((), (), s32[]{:S(2)}) async-start(), calls=%async_computation.9 | async-start | bytes 4194304 | tf_op jit(solution)/shard_map/psum | solution.py:145
  216.1 280.4 %all-gather.14.cloned.1.call-start = ((), (), s32[]{:S(2)}) async-start(), calls=%async_computation.10 | async-start | bytes 18874368 | tf_op jit(solution)/shard_map/all_gather | solution.py:160
  219.8 402.7 %all-gather.16.cloned.1.call-start = ((), (), s32[]{:S(2)}) async-start(), calls=%async_computation.11 | async-start | bytes 9437184 | tf_op jit(solution)/shard_map/all_gather | solution.py:161
  222.2 591.1 %all-reduce.12.cloned.1.call-start = ((), (), s32[]{:S(2)}) async-start(), calls=%async_computation.12 | async-start | bytes 4194304 | tf_op jit(solution)/shard_map/psum | solution.py:246
  699.3 167.9 %reduce-scatter.9.cloned.1.call-start = ((), (), s32[]{:S(2)}) async-start(), calls=%async_computation.14 | async-start | bytes 2621440 | tf_op jit(solution)/shard_map/reduce_scatter | solution.py:297
  825.6 87.3 %reduce-scatter.7.cloned.1.call-start = ((), (), s32[]{:S(2)}) async-start(), calls=%async_computation.13 | async-start | bytes 2621440 | tf_op jit(solution)/shard_map/reduce_scatter | solution.py:296
  834.1 182.5 %all-reduce.14.cloned.1.call-start = ((), (), s32[]{:S(2)}) async-start(), calls=%async_computation.19 | async-start | bytes 8388608 | tf_op jit(solution)/shard_map/psum | solution.py:200
  931.8 880.7 %reduce-scatter.17.cloned.1.call-start = ((), (), s32[]{:S(2)}) async-start(), calls=%async_computation.18 | async-start | bytes 56623104 | tf_op jit(solution)/shard_map/reduce_scatter | solution.py:238
  979.6 897.2 %reduce-scatter.15.cloned.1.call-start = ((), (), s32[]{:S(2)}) async-start(), calls=%async_computation.17 | async-start | bytes 73728 | tf_op jit(solution)/shard_map/reduce_scatter | solution.py:334
  982.1 985.9 %reduce-scatter.13.cloned.1.call-start = ((), (), s32[]{:S(2)}) async-start(), calls=%async_computation.16 | async-start | bytes 4718592 | tf_op jit(solution)/shard_map/reduce_scatter | solution.py:332
  986.7 1193.2 %reduce-scatter.11.cloned.1.call-start = ((), (), s32[]{:S(2)}) async-start(), calls=%async_computation.15 | async-start | bytes 14155776 | tf_op jit(solution)/shard_map/reduce_scatter | solution.py:331
  (78 other events, 985.8 us)
Sparse Core Ops, SparseCore 0:
  10.2 121.2 all-gather.7
  147.6 28.7 all-gather.11
  178.5 29.6 all-gather.9
  216.3 49.6 all-reduce.9
  268.8 227.7 all-gather.13
  499.4 123.1 all-gather.15
  699.5 49.5 all-reduce.11
  825.7 41.5 reduce-scatter.8
  869.7 43.1 reduce-scatter.6
  932.0 84.5 all-reduce.13
  1021.0 791.5 reduce-scatter.16
  1816.4 60.3 reduce-scatter.14
  1881.0 86.9 reduce-scatter.12
  1972.4 207.4 reduce-scatter.10
